TPU v7x, 256 devices: a whole 4x4x8 slice. The times are simulated.
256 devices in a mesh: elem: 64 (over y, z, core), snap: 4 (over x).
Axes of the slice: x: 4, y: 4, z: 8, core: 2. Of those that a mesh axis runs over, the one named last changes fastest.
Arguments:
- node_basis: bfloat16 [65536, 1536], P('elem'), may hold values from -0.25 to 0.25
- stiff_terms: bfloat16 [16, 24, 24], replicated, may hold values from -1.25 to 1.25
- reduced_coords: bfloat16 [512, 32], P(None, 'snap'), may hold values from -6 to 6
- sample_list: int32 [512], replicated, may hold values from 0 to 2047, as said below
- connectivity: int32 [2048, 8], replicated, may hold values from -1 to 65535, as said below
- node_slot: int32 [65536], replicated, may hold values from 0 to 65535, as said below
- elem_device: int32 [512], replicated, may hold values from 0 to 63, as said below
Outputs:
- ortho_panel: float32 [1024, 512, 512], P('elem', 'snap')
- triangle_factor: float32 [512, 512], P('elem')
Inputs may be any that keep to these rules, and one draw needn't show every extreme that they name: `sample_list`: distinct element ids. `connectivity`: each element lists 4, 6 or 8 live nodes first and -1 after them; the live nodes of one element are owned by distinct indices of elem (owner = node_slot // 1024); for every index d of elem and every owner o, at most 2 sampled elements computed on d have a live node owned by o, and some pair (d, o) reaches 2. `node_slot`: a permutation. `elem_device`: each index of elem computes at most 16 sampled elements; some index computes exactly 16.
All inputs are finite; a program needn't handle non-finite values.
Results may differ from a plain program's by a relative error of at most 0.0056.
Values may be sent and summed in bfloat16 or wider, within the bound.
A program may use at most 64 MiB of HBM per device.

v0:
```python
import jax
import jax.numpy as jnp
from jax import lax
from jax.sharding import PartitionSpec as P

MODES = 512
ENODES = 8
NDOF = 3


def shards(
    node_basis, stiff_terms, reduced_coords, sample_list, connectivity, node_slot, elem_device
):
    devices = lax.axis_size("elem")
    elem_rank = lax.axis_index("elem")
    node_rows = node_basis.shape[0]
    sampled = sample_list.shape[0]
    capacity = 2 * sampled // devices
    pair_bound = (capacity * ENODES + devices - 1) // devices
    node_ids = connectivity[sample_list]
    live_nodes = node_ids >= 0
    stored_rows = jnp.where(live_nodes, node_slot[jnp.maximum(node_ids, 0)], 0)
    owners = stored_rows // node_rows
    local_rows = stored_rows % node_rows
    position_ids = jnp.arange(sampled, dtype=jnp.int32)
    earlier = position_ids[None, :] < position_ids[:, None]
    same_device = elem_device[None, :] == elem_device[:, None]
    in_group = earlier & same_device
    slot_ids = jnp.sum(in_group.astype(jnp.int32), axis=1)
    owner_ids = jnp.arange(devices, dtype=jnp.int32)
    owned_mask = jnp.any(live_nodes[:, :, None] & (owners[:, :, None] == owner_ids), axis=1).astype(
        jnp.float32
    )
    ranks_by_owner = jnp.dot(
        in_group.astype(jnp.float32), owned_mask, precision=lax.Precision.HIGHEST
    ).astype(jnp.int32)
    peer_ranks = jnp.take_along_axis(ranks_by_owner, owners, axis=1)
    sending = live_nodes & (owners == elem_rank)
    target = jnp.where(sending, elem_device[:, None], devices)
    row_table = (
        jnp.full((devices, pair_bound), -1, jnp.int32)
        .at[target, peer_ranks]
        .set(local_rows, mode="drop")
    )
    send_rows = node_basis[jnp.maximum(row_table, 0)]
    outgoing = jnp.where((row_table >= 0)[:, :, None], send_rows, jnp.zeros((), jnp.bfloat16))
    incoming = lax.all_to_all(outgoing, "elem", split_axis=0, concat_axis=0, tiled=True)
    at_device = elem_device == elem_rank
    slot_index = jnp.where(at_device, slot_ids, capacity)
    slot_elem = (
        jnp.full((capacity,), sampled, jnp.int32).at[slot_index].set(position_ids, mode="drop")
    )
    slot_live = slot_elem < sampled
    picked = jnp.minimum(slot_elem, sampled - 1)
    slot_rows = incoming[owners[picked], jnp.minimum(peer_ranks[picked], pair_bound - 1)]
    slot_mask = live_nodes[picked] & slot_live[:, None]
    local_basis = jnp.where(slot_mask[:, :, None], slot_rows, jnp.zeros((), jnp.bfloat16))
    element_basis = local_basis.reshape(capacity, ENODES * NDOF, MODES)
    displaced = jnp.einsum(
        "ekm,ms->eks", element_basis, reduced_coords, preferred_element_type=jnp.float32
    ).astype(jnp.bfloat16)
    forces = jnp.einsum(
        "tkl,els->ekst", stiff_terms, displaced, preferred_element_type=jnp.float32
    ).astype(jnp.bfloat16)
    forces = forces.reshape(capacity, ENODES * NDOF, -1)
    projected = jnp.einsum(
        "ekm,ekc->emc", element_basis, forces, preferred_element_type=jnp.float32
    ).astype(jnp.bfloat16)
    banded = lax.all_to_all(projected, "snap", split_axis=1, concat_axis=2, tiled=True)
    band_rows = banded.reshape(-1, banded.shape[2])
    columns = band_rows.shape[1]
    total_rows = sampled * MODES
    partial_gram = lax.dot_general(
        band_rows, band_rows, (((0,), (0,)), ((), ())), preferred_element_type=jnp.float32
    )
    gram_matrix = lax.psum(partial_gram, ("elem", "snap"))
    gram_matrix = gram_matrix / total_rows
    lower_factor = jnp.linalg.cholesky(gram_matrix)
    identity_matrix = jnp.eye(columns, dtype=jnp.float32)
    lower_inverse = jax.scipy.linalg.solve_triangular(lower_factor, identity_matrix, lower=True)
    ortho_rows = lax.dot_general(
        band_rows.astype(jnp.float32),
        lower_inverse,
        (((1,), (1,)), ((), ())),
        precision=lax.Precision.HIGHEST,
        preferred_element_type=jnp.float32,
    )
    share = columns // devices
    upper_rows = lax.dynamic_slice_in_dim(lower_factor.T, elem_rank * share, share, 0)
    return (ortho_rows.reshape(banded.shape), upper_rows)


def solution(mesh):
    placed = (P("elem", None), P(), P(None, "snap"), P(), P(), P(), P())
    return jax.shard_map(
        shards,
        mesh=mesh,
        in_specs=placed,
        out_specs=(P("elem", "snap", None), P("elem", None)),
        check_vma=False,
    )
```

profile of v0, /device:TPU:2, one launch (start us, length us, event | category | flops | bytes accessed | tf_op | source)
XLA Modules:
  0.0 630.0 jit_solution(7660797386319666554)
XLA Ops:
  8.0 2.3 copy.109
  10.3 2.9 gather_fusion
  15.9 23.0 %gather_fusion.2 = s32[4096]{0:T(1024)S(1)} fusion(s32[65536]{0:T(1024)S(1)} %copy-done.1, s32[4096]{0:T(1024)S(1)} %broadcast_clamp_fusion), kind=kCustom, calls=%fused_computation.2 | custom fusion | bytes 49152 | tf_op jit(solution)/shard_map/gather | solution.py:22
  48.0 33.0 %gather_fusion.7 = s32[4096]{0:T(1024)S(1)} fusion(s32[512,64]{0,1:T(8,128)S(1)} %convolution_convert_fusion.2, s32[4096]{0:T(1024)S(1)} %reshape.363), kind=kCustom, calls=%fused_computation.7 | custom fusion | bytes 65536 | tf_op jit(solution)/shard_map/jit(take_along_axis)/gather | solution.py:37
  88.4 15.5 %scatter_custom_fusion.1 = s32[128]{0:T(128)S(1)} fusion(s32[4096]{0:T(1024)S(1)} %reshape.377, s32[4096]{0:T(1024)S(1)} %reshape.379, s32[]{:T(128)} %constant.211.clone.1), kind=kCustom, calls=%fused_computation.155 | custom fusion | bytes 516
  109.7 12.1 %all-to-all-start = ((bf16[64,2,1536]{2,1,0:T(2,128)(2,1)}), bf16[64,2,1536]{2,1,0:T(2,128)(2,1)S(1)}, u32[]{:S(2)}, u32[]{:S(2)}) async-start(bf16[64,2,1536]{2,1,0:T(2,128)(2,1)} %broadcast_select_fusion), calls=%async_computation | async-start | bytes 786432 | tf_op jit(solution)/shard_map/all_to_all | solution.py:47
  124.7 3.2 scatter_custom_fusion
  132.6 2.2 gather_fusion.4
  142.2 2.3 gather_fusion.6
  151.1 29.8 %all_to_all.20 = bf16[16,512,128]{2,0,1:T(8,128)(2,1)} all-to-all(bf16[16,512,128]{2,0,1:T(8,128)(2,1)S(1)} %copy.125), channel_id=1, replica_groups=mesh['elem'=64,'snap'=4] {'snap'}, dimensions={1} | all-to-all | bytes 4194304 | tf_op jit(solution)/shard_map/all_to_all | solution.py:69
  180.9 5.1 copy.126
  186.0 4.5 fusion
  192.4 4.5 copy.127
  197.0 4.3 dot_general.24
  201.3 248.6 %all-reduce.3.cloned.1.call-done = f32[512,512]{0,1:T(8,128)} async-done(((f32[512,512]{0,1:T(8,128)}), f32[512,512]{0,1:T(8,128)}) %all-reduce.3.cloned.1.call-update) | async-done | bytes 1048592 | tf_op jit(solution)/shard_map/psum | solution.py:76
  449.8 2.3 broadcast_multiply_fusion
  452.1 2.5 copy.129
  457.4 11.7 %cholesky.104 = f32[128,128]{1,0:T(8,128)S(1)} custom-call(f32[128,128]{1,0:T(8,128)S(1)} %cholesky.266), custom_call_target="Cholesky" | custom-call | tf_op jit(solution)/shard_map/jit(cholesky)/cholesky | solution.py:78
  469.7 9.8 %custom-call.31 = f32[1,128,128]{1,2,0:T(8,128)S(1)} custom-call(f32[1,128,128]{2,1,0:T(8,128)S(1)} %get-tuple-element.47), custom_call_target="InvertDiagBlocksLowerTriangular" | custom-call | tf_op jit(solution)/shard_map/jit(cholesky)/cholesky | solution.py:78
  484.0 11.7 %cholesky.217 = f32[128,128]{1,0:T(8,128)S(1)} custom-call(f32[128,128]{1,0:T(8,128)S(1)} %cholesky.270), custom_call_target="Cholesky" | custom-call | tf_op jit(solution)/shard_map/jit(cholesky)/cholesky | solution.py:78
  499.0 10.2 %custom-call.32 = f32[1,128,128]{1,2,0:T(8,128)S(1)} custom-call(f32[1,128,128]{2,1,0:T(8,128)S(1)} %get-tuple-element.44), custom_call_target="InvertDiagBlocksLowerTriangular" | custom-call | tf_op jit(solution)/shard_map/jit(cholesky)/cholesky | solution.py:78
  512.5 11.7 %cholesky.238 = f32[128,128]{1,0:T(8,128)S(1)} custom-call(f32[128,128]{1,0:T(8,128)S(1)} %cholesky.275), custom_call_target="Cholesky" | custom-call | tf_op jit(solution)/shard_map/jit(cholesky)/cholesky | solution.py:78
  525.5 9.8 %custom-call.33 = f32[1,128,128]{1,2,0:T(8,128)S(1)} custom-call(f32[1,128,128]{2,1,0:T(8,128)S(1)} %get-tuple-element.41), custom_call_target="InvertDiagBlocksLowerTriangular" | custom-call | tf_op jit(solution)/shard_map/jit(cholesky)/cholesky | solution.py:78
  537.6 11.9 %cholesky.255 = f32[128,128]{1,0:T(8,128)S(1)} custom-call(f32[128,128]{1,0:T(8,128)S(1)} %convolution_subtract_fusion.5), custom_call_target="Cholesky" | custom-call | tf_op jit(solution)/shard_map/jit(cholesky)/cholesky | solution.py:78
  553.9 2.5 fusion.12
  557.2 13.5 %while.1 = (s32[]{:T(128)}, f32[512,512]{1,0:T(8,128)}, s32[4,2]{0,1:T(2,128)S(1)}, f32[4,128,128]{2,1,0:T(8,128)}, s32[]{:T(128)}) while((s32[]{:T(128)}, f32[512,512]{1,0:T(8,128)}, s32[4,2]{0,1:T(2,128)S(1)}, f32[4,128,128]{2,1,0:T(8,128)}, s32[]{:T(128)}) %tuple.39), condition=%wide.while_cond, body=%wide.while_body.sunk | while | flops 2 | bytes 132205 | solution.py:80
  557.8 2.8 bitcast_dynamic-update-slice_fusion.2
  561.2 2.8 bitcast_dynamic-update-slice_fusion.2
  564.6 2.8 bitcast_dynamic-update-slice_fusion.2
  568.0 2.7 bitcast_dynamic-update-slice_fusion.2
  570.7 40.1 %custom-call.34 = f32[4,128,128]{1,2,0:T(8,128)S(1)} custom-call(f32[4,128,128]{2,1,0:T(8,128)} %get-tuple-element.9), custom_call_target="InvertDiagBlocksLowerTriangular" | custom-call | tf_op jit(solution)/shard_map/jit(_solve_triangular)/triangular_solve | solution.py:80
  617.9 5.1 fusion.4
  (129 shorter events, 79.1 us)
Async XLA Ops:
  7.2 97.9 %copy-start = (bf16[1024,1536]{1,0:T(8,128)(2,1)S(1)}, bf16[1024,1536]{1,0:T(8,128)(2,1)}, u32[]{:S(2)}) copy-start(bf16[1024,1536]{1,0:T(8,128)(2,1)} %param.7) | copy-start | bytes 9437188
  8.0 7.9 %copy-start.1 = (s32[65536]{0:T(1024)S(1)}, s32[65536]{0:T(1024)}, u32[]{:S(2)}) copy-start(s32[65536]{0:T(1024)} %param.12) | copy-start | bytes 786436
  39.0 8.6 %copy-start.8 = (s32[512]{0:T(512)S(1)}, s32[512]{0:T(512)}, u32[]{:S(2)}) copy-start(s32[512]{0:T(512)} %param.13) | copy-start | bytes 6148
  40.0 1.9 copy-start.5
  41.9 40.0 %copy-start.6 = (pred[512,8]{1,0:T(8,128)(4,1)}, pred[512,8]{1,0:T(8,128)(4,1)S(1)}, u32[]{:S(2)}) copy-start(pred[512,8]{1,0:T(8,128)(4,1)S(1)} %get-tuple-element.33) | copy-start | bytes 12292
  43.1 1.3 copy-start.4
  47.9 38.2 %copy-start.10 = (s32[2]{0:T(128)S(1)}, s32[2]{0:T(128)}, u32[]{:S(2)}) copy-start(s32[2]{0:T(128)} %constant.235) | copy-start | bytes 28
  48.0 38.2 %copy-start.9 = (s32[2]{0:T(128)S(1)}, s32[2]{0:T(128)}, u32[]{:S(2)}) copy-start(s32[2]{0:T(128)} %constant.232) | copy-start | bytes 28
  109.7 32.5 %all-to-all-start = ((bf16[64,2,1536]{2,1,0:T(2,128)(2,1)}), bf16[64,2,1536]{2,1,0:T(2,128)(2,1)S(1)}, u32[]{:S(2)}, u32[]{:S(2)}) async-start(bf16[64,2,1536]{2,1,0:T(2,128)(2,1)} %broadcast_select_fusion), calls=%async_computation | async-start | bytes 786432 | tf_op jit(solution)/shard_map/all_to_all | solution.py:47
  121.8 328.0 %all-reduce.3.cloned.1.call-start = ((), (), s32[]{:S(2)}) async-start(), calls=%async_computation.2 | async-start | bytes 2097152 | tf_op jit(solution)/shard_map/psum | solution.py:76
  456.4 1.0 copy-start.3
  469.1 0.6 copy-start.7
  613.3 4.6 copy-start.2
Sparse Core Ops, SparseCore 0:
  190.6 259.1 all-reduce.2
where the time goes:
time: 638 us; the launch traced here: 630 us
  waiting for transfers between devices  249 us (39%)
  other arithmetic  149 us (23%)
  local copies, waits for them, and re-layouts  143 us (22%)
  matrix products  29.9 us (5%)
  blocking collectives  29.8 us (5%)
  between operations  17.2 us (3%)
  starting transfers between devices  12.1 us (2%)
    psum x1, waiting for transfers between devices, shards(): gram_matrix = lax.psum(partial_gram, ('elem', 'snap'))  249 us
    another operation x14, other arithmetic, shards(): lower_factor = jnp.linalg.cholesky(gram_matrix)  80.7 us
    another operation x3, other arithmetic, shards(): jax.scipy.linalg.solve_triangular(lower_factor, identity_matrix, lower=True)  42.6 us
    gather x4, local copies, waits for them, and re-layouts, shards(): peer_ranks = jnp.take_along_axis(ranks_by_owner, owners, axis=1)  35.9 us
    all_to_all x1, blocking collectives, shards(): lax.all_to_all(projected, 'snap', split_axis=1, concat_axis=2, tiled=True)  29.8 us
    gather x3, local copies, waits for them, and re-layouts, shards(): stored_rows = jnp.where(live_nodes, node_slot[jnp.maximum(node_ids, 0)], 0)  24.1 us
    unnamed x28, local copies, waits for them, and re-layouts  21.4 us
    another operation x12, local copies, waits for them, and re-layouts  13.5 us
  transfers between devices with their start and end apart: 2, of which 1 were waited for; matrix products, arithmetic and copies ran while one was open for 5% of the time, Pallas kernels for 0%

commit v1 on v0

--- a/solution.py
+++ b/solution.py
@@ -73,7 +73,12 @@
     partial_gram = lax.dot_general(
         band_rows, band_rows, (((0,), (0,)), ((), ())), preferred_element_type=jnp.float32
     )
-    gram_matrix = lax.psum(partial_gram, ("elem", "snap"))
+
+    def remake_sums_all(panel, device_axis, row_axis):
+        ready = lax.psum(panel, device_axis)
+        return lax.psum(ready, row_axis)
+
+    gram_matrix = remake_sums_all(partial_gram, "elem", "snap")
     gram_matrix = gram_matrix / total_rows
     lower_factor = jnp.linalg.cholesky(gram_matrix)
     identity_matrix = jnp.eye(columns, dtype=jnp.float32)

time: 638 us -> 618 us (0.969)
  waiting for transfers between devices: 249 us -> 227 us
    psum x1 -> x2, waiting for transfers between devices: 249 us -> 227 us  [the longest x1 188 us: remake_sums_all(): ready = lax.psum(panel, device_axis)]
  transfers between devices with their start and end apart: 2 -> 3, of which waited for: 1 -> 2; matrix products, arithmetic and copies ran while one was open for 5% -> 5% of each run, Pallas kernels for 0% -> 0%
where the time goes in v1:
time: 618 us; the launch traced here: 609 us
  waiting for transfers between devices  227 us (37%)
  other arithmetic  149 us (24%)
  local copies, waits for them, and re-layouts  143 us (23%)
  matrix products  29.9 us (5%)
  blocking collectives  29.8 us (5%)
  between operations  17.2 us (3%)
  starting transfers between devices  12.2 us (2%)
    psum x1, waiting for transfers between devices, remake_sums_all(): ready = lax.psum(panel, device_axis)  188 us
    another operation x14, other arithmetic, shards(): lower_factor = jnp.linalg.cholesky(gram_matrix)  80.7 us
    another operation x3, other arithmetic, shards(): jax.scipy.linalg.solve_triangular(lower_factor, identity_matrix, lower=True)  42.6 us
    psum x1, waiting for transfers between devices, remake_sums_all(): return lax.psum(ready, row_axis)  39.1 us
    gather x4, local copies, waits for them, and re-layouts, shards(): peer_ranks = jnp.take_along_axis(ranks_by_owner, owners, axis=1)  35.9 us
    all_to_all x1, blocking collectives, shards(): lax.all_to_all(projected, 'snap', split_axis=1, concat_axis=2, tiled=True)  29.8 us
    gather x3, local copies, waits for them, and re-layouts, shards(): stored_rows = jnp.where(live_nodes, node_slot[jnp.maximum(node_ids, 0)], 0)  24.1 us
    unnamed x28, local copies, waits for them, and re-layouts  21.4 us
  transfers between devices with their start and end apart: 3, of which 2 were waited for; matrix products, arithmetic and copies ran while one was open for 5% of the time, Pallas kernels for 0%

profile of v1, /device:TPU:2, one launch (start us, length us, event | category | flops | bytes accessed | tf_op | source)
XLA Modules:
  0.0 608.7 jit_solution(494993440375793531)
XLA Ops:
  8.0 2.3 copy.109
  10.3 2.9 gather_fusion
  15.9 23.0 %gather_fusion.2 = s32[4096]{0:T(1024)S(1)} fusion(s32[65536]{0:T(1024)S(1)} %copy-done.1, s32[4096]{0:T(1024)S(1)} %broadcast_clamp_fusion), kind=kCustom, calls=%fused_computation.2 | custom fusion | bytes 49152 | tf_op jit(solution)/shard_map/gather | solution.py:22
  48.0 33.0 %gather_fusion.7 = s32[4096]{0:T(1024)S(1)} fusion(s32[512,64]{0,1:T(8,128)S(1)} %convolution_convert_fusion.2, s32[4096]{0:T(1024)S(1)} %reshape.363), kind=kCustom, calls=%fused_computation.7 | custom fusion | bytes 65536 | tf_op jit(solution)/shard_map/jit(take_along_axis)/gather | solution.py:37
  88.4 15.5 %scatter_custom_fusion.1 = s32[128]{0:T(128)S(1)} fusion(s32[4096]{0:T(1024)S(1)} %reshape.377, s32[4096]{0:T(1024)S(1)} %reshape.379, s32[]{:T(128)} %constant.211.clone.1), kind=kCustom, calls=%fused_computation.155 | custom fusion | bytes 516
  109.7 12.1 %all-to-all-start = ((bf16[64,2,1536]{2,1,0:T(2,128)(2,1)}), bf16[64,2,1536]{2,1,0:T(2,128)(2,1)S(1)}, u32[]{:S(2)}, u32[]{:S(2)}) async-start(bf16[64,2,1536]{2,1,0:T(2,128)(2,1)} %broadcast_select_fusion), calls=%async_computation | async-start | bytes 786432 | tf_op jit(solution)/shard_map/all_to_all | solution.py:47
  124.7 3.2 scatter_custom_fusion
  142.2 2.3 gather_fusion.6
  151.1 29.8 %all_to_all.20 = bf16[16,512,128]{2,0,1:T(8,128)(2,1)} all-to-all(bf16[16,512,128]{2,0,1:T(8,128)(2,1)S(1)} %copy.125), channel_id=1, replica_groups=mesh['elem'=64,'snap'=4] {'snap'}, dimensions={1} | all-to-all | bytes 4194304 | tf_op jit(solution)/shard_map/all_to_all | solution.py:69
  180.9 5.1 copy.126
  186.0 4.5 fusion
  190.6 188.0 %all-reduce.4.cloned.1.call-done = f32[512,512]{0,1:T(8,128)} async-done(((f32[512,512]{0,1:T(8,128)}), f32[512,512]{0,1:T(8,128)}) %all-reduce.4.cloned.1.call-update) | async-done | bytes 1048592 | tf_op jit(solution)/shard_map/psum | solution.py:78
  380.5 4.5 copy.127
  385.1 4.3 dot_general.24
  389.4 39.1 %all-reduce.6.cloned.1.call-done = f32[512,512]{0,1:T(8,128)} async-done(((f32[512,512]{0,1:T(8,128)}), f32[512,512]{0,1:T(8,128)}) %all-reduce.6.cloned.1.call-update) | async-done | bytes 1048592 | tf_op jit(solution)/shard_map/psum | solution.py:79
  428.4 2.3 broadcast_multiply_fusion
  430.7 2.5 copy.129
  436.0 11.7 %cholesky.104 = f32[128,128]{1,0:T(8,128)S(1)} custom-call(f32[128,128]{1,0:T(8,128)S(1)} %cholesky.266), custom_call_target="Cholesky" | custom-call | tf_op jit(solution)/shard_map/jit(cholesky)/cholesky | solution.py:83
  448.4 9.8 %custom-call.31 = f32[1,128,128]{1,2,0:T(8,128)S(1)} custom-call(f32[1,128,128]{2,1,0:T(8,128)S(1)} %get-tuple-element.47), custom_call_target="InvertDiagBlocksLowerTriangular" | custom-call | tf_op jit(solution)/shard_map/jit(cholesky)/cholesky | solution.py:83
  462.6 11.7 %cholesky.217 = f32[128,128]{1,0:T(8,128)S(1)} custom-call(f32[128,128]{1,0:T(8,128)S(1)} %cholesky.270), custom_call_target="Cholesky" | custom-call | tf_op jit(solution)/shard_map/jit(cholesky)/cholesky | solution.py:83
  477.6 10.2 %custom-call.32 = f32[1,128,128]{1,2,0:T(8,128)S(1)} custom-call(f32[1,128,128]{2,1,0:T(8,128)S(1)} %get-tuple-element.44), custom_call_target="InvertDiagBlocksLowerTriangular" | custom-call | tf_op jit(solution)/shard_map/jit(cholesky)/cholesky | solution.py:83
  491.1 11.7 %cholesky.238 = f32[128,128]{1,0:T(8,128)S(1)} custom-call(f32[128,128]{1,0:T(8,128)S(1)} %cholesky.275), custom_call_target="Cholesky" | custom-call | tf_op jit(solution)/shard_map/jit(cholesky)/cholesky | solution.py:83
  504.1 9.8 %custom-call.33 = f32[1,128,128]{1,2,0:T(8,128)S(1)} custom-call(f32[1,128,128]{2,1,0:T(8,128)S(1)} %get-tuple-element.41), custom_call_target="InvertDiagBlocksLowerTriangular" | custom-call | tf_op jit(solution)/shard_map/jit(cholesky)/cholesky | solution.py:83
  516.2 11.9 %cholesky.255 = f32[128,128]{1,0:T(8,128)S(1)} custom-call(f32[128,128]{1,0:T(8,128)S(1)} %convolution_subtract_fusion.5), custom_call_target="Cholesky" | custom-call | tf_op jit(solution)/shard_map/jit(cholesky)/cholesky | solution.py:83
  532.5 2.5 fusion.12
  535.8 13.5 %while.1 = (s32[]{:T(128)}, f32[512,512]{1,0:T(8,128)}, s32[4,2]{0,1:T(2,128)S(1)}, f32[4,128,128]{2,1,0:T(8,128)}, s32[]{:T(128)}) while((s32[]{:T(128)}, f32[512,512]{1,0:T(8,128)}, s32[4,2]{0,1:T(2,128)S(1)}, f32[4,128,128]{2,1,0:T(8,128)}, s32[]{:T(128)}) %tuple.39), condition=%wide.while_cond, body=%wide.while_body.sunk | while | flops 2 | bytes 132205 | solution.py:85
  536.4 2.8 bitcast_dynamic-update-slice_fusion.2
  539.8 2.8 bitcast_dynamic-update-slice_fusion.2
  543.2 2.8 bitcast_dynamic-update-slice_fusion.2
  546.6 2.7 bitcast_dynamic-update-slice_fusion.2
  549.3 40.1 %custom-call.34 = f32[4,128,128]{1,2,0:T(8,128)S(1)} custom-call(f32[4,128,128]{2,1,0:T(8,128)} %get-tuple-element.9), custom_call_target="InvertDiagBlocksLowerTriangular" | custom-call | tf_op jit(solution)/shard_map/jit(_solve_triangular)/triangular_solve | solution.py:85
  596.5 5.1 fusion.4
  (132 shorter events, 81.4 us)
Async XLA Ops:
  7.2 97.9 %copy-start = (bf16[1024,1536]{1,0:T(8,128)(2,1)S(1)}, bf16[1024,1536]{1,0:T(8,128)(2,1)}, u32[]{:S(2)}) copy-start(bf16[1024,1536]{1,0:T(8,128)(2,1)} %param.7) | copy-start | bytes 9437188
  8.0 7.9 %copy-start.1 = (s32[65536]{0:T(1024)S(1)}, s32[65536]{0:T(1024)}, u32[]{:S(2)}) copy-start(s32[65536]{0:T(1024)} %param.12) | copy-start | bytes 786436
  39.0 8.6 %copy-start.8 = (s32[512]{0:T(512)S(1)}, s32[512]{0:T(512)}, u32[]{:S(2)}) copy-start(s32[512]{0:T(512)} %param.13) | copy-start | bytes 6148
  40.0 1.9 copy-start.5
  41.9 40.0 %copy-start.6 = (pred[512,8]{1,0:T(8,128)(4,1)}, pred[512,8]{1,0:T(8,128)(4,1)S(1)}, u32[]{:S(2)}) copy-start(pred[512,8]{1,0:T(8,128)(4,1)S(1)} %get-tuple-element.33) | copy-start | bytes 12292
  43.1 1.3 copy-start.4
  47.9 38.2 %copy-start.10 = (s32[2]{0:T(128)S(1)}, s32[2]{0:T(128)}, u32[]{:S(2)}) copy-start(s32[2]{0:T(128)} %constant.235) | copy-start | bytes 28
  48.0 38.2 %copy-start.9 = (s32[2]{0:T(128)S(1)}, s32[2]{0:T(128)}, u32[]{:S(2)}) copy-start(s32[2]{0:T(128)} %constant.232) | copy-start | bytes 28
  109.7 32.5 %all-to-all-start = ((bf16[64,2,1536]{2,1,0:T(2,128)(2,1)}), bf16[64,2,1536]{2,1,0:T(2,128)(2,1)S(1)}, u32[]{:S(2)}, u32[]{:S(2)}) async-start(bf16[64,2,1536]{2,1,0:T(2,128)(2,1)} %broadcast_select_fusion), calls=%async_computation | async-start | bytes 786432 | tf_op jit(solution)/shard_map/all_to_all | solution.py:47
  121.8 256.7 %all-reduce.4.cloned.1.call-start = ((), (), s32[]{:S(2)}) async-start(), calls=%async_computation.2 | async-start | bytes 2097152 | tf_op jit(solution)/shard_map/psum | solution.py:78
  190.5 237.9 %all-reduce.6.cloned.1.call-start = ((), (), s32[]{:S(2)}) async-start(), calls=%async_computation.3 | async-start | bytes 2097152 | tf_op jit(solution)/shard_map/psum | solution.py:79
  435.1 1.0 copy-start.3
  447.7 0.6 copy-start.7
  591.9 4.6 copy-start.2
Sparse Core Ops, SparseCore 0:
  190.6 187.8 all-reduce.3
  380.9 47.4 all-reduce.5
